TPU v7x, 128 devices: a whole 4x4x4 slice. The times are simulated.
128 devices in a mesh: dp: 8 (over x, y_hi), seq: 16 (over y_lo, z, core).
Axes of the slice: x: 4, y: 4 (y_hi: 2, y_lo: 2; y = y_hi * 2 + y_lo), z: 4, core: 2. Of those that a mesh axis runs over, the one named last changes fastest.
Arguments:
- caption_states: bfloat16 [8, 128, 4096], P('dp', None, 'seq'), may hold values from -1600 to 1600
- caption_gain: float32 [4096], P('seq'), may hold values from 0.25 to 2.5
- text_proj: bfloat16 [4096, 4608], P('seq'), may hold values from -0.09375 to 0.09375
- caption_len: int32 [8], P('dp'), may hold values from 1 to 128, 640 in all
- slot_source: int32 [8, 128], P('dp'), may hold values from 0 to 127, each once within a row
- query_gain: float32 [128], replicated, may hold values from 0.5 to 2
- key_gain: float32 [128], replicated, may hold values from 0.5 to 2
- image_q: bfloat16 [8, 2048, 1536], P('dp', 'seq'), may hold values from -34 to 34
- image_k: bfloat16 [8, 2048, 1536], P('dp', 'seq'), may hold values from -6.5 to 6.5
- image_v: bfloat16 [8, 2048, 1536], P('dp', 'seq'), may hold values from -6 to 6
- out_weight: bfloat16 [3072, 1536], replicated, may hold values from -0.15625 to 0.15625
- gate: float32 [8, 3072], P('dp'), may hold values from -4 to 4
- d_out: bfloat16 [8, 2048, 3072], P('dp', 'seq'), may hold values from -2.5 to 2.5
Outputs:
- image_out: bfloat16 [8, 2048, 3072], P('dp', 'seq')
- text_attn: bfloat16 [8, 128, 1536], P('dp', 'seq')
- d_attn: bfloat16 [8, 2048, 1536], P('dp', 'seq')
- grad_wo: float32 [3072, 1536], P(('dp', 'seq'))
- grad_gate: float32 [8, 3072], P('dp', 'seq')
Inputs may be any that keep to these rules, and one draw needn't show every extreme that they name: `caption_len`: caption lengths in tokens; the longest is 128. `slot_source`: each row is a permutation: every caption row of the sequence sits in exactly one slot; slots whose row is not below the caption's length are padding.
All inputs are finite; a program needn't handle non-finite values. No bound on the sum of `caption_len` on one device may be relied on, other than what follows from the above.
Results may differ from a plain program's by a relative error of at most 0.0095.
Values may be sent and summed in bfloat16 or wider, within the bound.
A program may use at most 128 MiB of HBM per device.

v0:
```python
import jax
import jax.numpy as jnp
from jax import lax
from jax.sharding import PartitionSpec as P

DT5 = 4096
neg_big = -1e30
eps_norm = 1e-06


def head_norm(values_in, gain_vec):
    shaped = values_in.reshape(values_in.shape[0], -1, gain_vec.shape[0])
    normed = (
        shaped * lax.rsqrt(jnp.mean(shaped * shaped, axis=-1, keepdims=True) + eps_norm) * gain_vec
    )
    return normed.reshape(values_in.shape).astype(jnp.bfloat16)


def text_heads(summed, squares, query_gain, key_gain, inner_width):
    factor = lax.rsqrt(squares / DT5 + eps_norm)
    normed = summed * factor[:, None]
    text_query = head_norm(normed[:, :inner_width], query_gain)
    text_key = head_norm(normed[:, inner_width : 2 * inner_width], key_gain)
    text_value = normed[:, 2 * inner_width :].astype(jnp.bfloat16)
    return (text_query, text_key, text_value)


def start_state(query_heads):
    query_count, head_count, head_size = query_heads.shape
    return (
        jnp.full((head_count, query_count), neg_big, jnp.float32),
        jnp.zeros((head_count, query_count), jnp.float32),
        jnp.zeros((head_count, query_count, head_size), jnp.float32),
    )


def attend(running, query_heads, key_rows, value_rows, usable):
    max_old, total_old, weighted = running
    count_keys = key_rows.shape[0]
    head_size = query_heads.shape[2]
    key_heads = key_rows.reshape(count_keys, -1, head_size)
    value_heads = value_rows.reshape(count_keys, -1, head_size)
    scores = jnp.einsum(
        "qhd,khd->hqk", query_heads, key_heads, preferred_element_type=jnp.float32
    ) * head_size ** (-0.5)
    scores = jnp.where(usable[None, None, :], scores, neg_big)
    max_new = jnp.maximum(max_old, jnp.max(scores, axis=-1))
    weights_now = jnp.where(usable[None, None, :], jnp.exp(scores - max_new[..., None]), 0.0)
    total_new = jnp.sum(weights_now, axis=-1)
    weighted = jnp.einsum(
        "hqk,khd->hqd",
        weights_now.astype(jnp.bfloat16),
        value_heads,
        preferred_element_type=jnp.float32,
    )
    return (max_new, total_new, weighted)


def on_device(
    caption_states,
    caption_gain,
    text_proj,
    caption_len,
    slot_source,
    query_gain,
    key_gain,
    image_q,
    image_k,
    image_v,
    out_weight,
    gate,
    d_out,
):
    seq_count = lax.axis_size("seq")
    seq_index = lax.axis_index("seq")
    slot_total = slot_source.shape[1]
    slot_local = slot_total // seq_count
    image_local = image_q.shape[1]
    inner_width = image_q.shape[2]
    head_size = query_gain.shape[0]
    sources = slot_source[0]
    picked = jnp.take(caption_states[0], sources, axis=0).astype(jnp.float32)
    scaled_rows = (picked * caption_gain).astype(jnp.bfloat16)
    partial_proj = jnp.dot(scaled_rows, text_proj, preferred_element_type=jnp.float32)
    partial_squares = jnp.sum(picked * picked, axis=1)
    usable_slots = sources < caption_len[0]
    own_usable = lax.dynamic_slice_in_dim(usable_slots, seq_index * slot_local, slot_local)
    summed, squares = (
        lax.psum_scatter(partial_proj, "seq", scatter_dimension=0, tiled=True),
        lax.psum_scatter(partial_squares, "seq", scatter_dimension=0, tiled=True),
    )
    text_query, text_key, text_value = text_heads(
        summed, squares, query_gain, key_gain, inner_width
    )
    queries = jnp.concatenate([image_q[0], text_query], axis=0)
    query_heads = queries.reshape(queries.shape[0], -1, head_size)
    key_rows = jnp.concatenate([image_k[0], text_key], axis=0)
    value_rows = jnp.concatenate([image_v[0], text_value], axis=0)
    usable_all = jnp.concatenate(
        [
            jnp.ones((seq_count, image_local), dtype=jnp.bool_),
            usable_slots.reshape(seq_count, slot_local),
        ],
        axis=1,
    ).reshape(-1)
    running = attend(
        start_state(query_heads),
        query_heads,
        lax.all_gather(key_rows, "seq", axis=0, tiled=True),
        lax.all_gather(value_rows, "seq", axis=0, tiled=True),
        usable_all,
    )
    max_final, total_final, weighted = running
    attention = (
        jnp.transpose(weighted / total_final[..., None], (1, 0, 2))
        .reshape(-1, inner_width)
        .astype(jnp.bfloat16)
    )
    image_attn = attention[:image_local]
    text_attn = jnp.where(own_usable[:, None], attention[image_local:], jnp.zeros((), jnp.bfloat16))
    projected = lax.dot_general(
        image_attn, out_weight, (((1,), (1,)), ((), ())), preferred_element_type=jnp.float32
    )
    gate_row = gate[0]
    image_out = (gate_row * projected).astype(jnp.bfloat16)
    cotangent = d_out[0].astype(jnp.float32)
    gated_grad = (gate_row * cotangent).astype(jnp.bfloat16)
    gate_term = jnp.sum(projected * cotangent, axis=0)
    d_attn = jnp.dot(gated_grad, out_weight, preferred_element_type=jnp.float32).astype(
        jnp.bfloat16
    )
    grad_wo = lax.psum_scatter(
        lax.dot_general(
            gated_grad, image_attn, (((0,), (0,)), ((), ())), preferred_element_type=jnp.float32
        ),
        ("dp", "seq"),
        scatter_dimension=0,
        tiled=True,
    )
    grad_gate = lax.psum_scatter(gate_term, "seq", scatter_dimension=0, tiled=True)
    return (image_out[None], text_attn[None], d_attn[None], grad_wo, grad_gate[None])


def solution(mesh):
    in_specs = (
        P("dp", None, "seq"),
        P("seq"),
        P("seq", None),
        P("dp"),
        P("dp", None),
        P(),
        P(),
        P("dp", "seq", None),
        P("dp", "seq", None),
        P("dp", "seq", None),
        P(),
        P("dp", None),
        P("dp", "seq", None),
    )
    out_specs = (
        P("dp", "seq", None),
        P("dp", "seq", None),
        P("dp", "seq", None),
        P(("dp", "seq"), None),
        P("dp", "seq"),
    )
    return jax.shard_map(
        on_device, mesh=mesh, in_specs=in_specs, out_specs=out_specs, check_vma=False
    )
```

profile of v0, /device:TPU:0, one launch (start us, length us, event | category | flops | bytes accessed | tf_op | source)
XLA Modules:
  0.0 446.3 jit_solution(14536937245673772686)
XLA Ops:
  8.1 0.7 fusion.38
  9.5 1.6 gather_fusion
  11.1 2.6 fusion.28
  13.8 1.2 dynamic-slice
  15.9 31.7 %all-reduce.1 = f32[128]{0:T(128)S(1)} all-reduce(f32[128]{0:T(128)S(1)} %fusion.27), channel_id=3, replica_groups=mesh['dp'=8,'seq'=16] {'seq'}, use_global_device_ids=true, to_apply=%region_2.3.clone | all-reduce | flops 128 | bytes 1024
  47.7 0.7 broadcast_bitcast_fusion
  48.3 32.1 %reduce-scatter.3.cloned.1.call-done = f32[8,4608]{1,0:T(8,128)} async-done(((f32[128,4608]{1,0:T(8,128)}), f32[8,4608]{1,0:T(8,128)}) %reduce-scatter.3.cloned.1.call-update) | async-done | bytes 147472 | tf_op jit(solution)/shard_map/reduce_scatter | solution.py:89
  80.4 1.0 broadcast_multiply_fusion
  81.6 1.8 pad_maximum_fusion
  83.5 0.8 pad_maximum_fusion.1
  85.1 40.8 %all-gather.3.cloned.1.call-done = bf16[2176,1536]{1,0:T(8,128)(2,1)} async-done(((bf16[136,1536]{1,0:T(8,128)(2,1)}), bf16[2176,1536]{1,0:T(8,128)(2,1)}) %all-gather.3.cloned.1.call-update) | async-done | bytes 6684688 | tf_op jit(solution)/shard_map/all_gather | solution.py:109
  125.9 9.3 %copy.29 = bf16[2176,1536]{0,1:T(8,128)(2,1)} copy(bf16[2176,1536]{1,0:T(8,128)(2,1)} %all-gather.3.cloned.1.call-done) | data formatting | bytes 13369344 | tf_op jit(solution)/shard_map/all_gather | solution.py:109
  135.3 4.8 %fusion = (f32[12,136]{1,0:T(8,128)S(1)}, f32[12,136,2176]{2,1,0:T(8,128)S(1)}) fusion(pred[2176]{0:T(1024)(128)(4,1)S(1)} %broadcast_in_dim.67, bf16[2176,12,128]{0,2,1:T(8,128)(2,1)} %bitcast.78, bf16[8,12,128]{2,0,1:T(8,128)(2,1)S(1)} %get-tuple-element.9, bf16[128,12,128]{2,0,1:T(8,128)(2,1)S(1)} %copy.28), kind=kOutput, calls=%fused_computation.3 | convolution fusion | flops 920603008 | bytes 21316096 | tf_op jit(solution)/shard_map/qhd,khd->hqk/dot_general | solution.py:43
  140.1 5.1 %copy-done.2 = f32[12,136,2176]{2,1,0:T(8,128)} copy-done((f32[12,136,2176]{2,1,0:T(8,128)}, f32[12,136,2176]{2,1,0:T(8,128)S(1)}, u32[]{:S(2)}) %copy-start.2) | copy-done | bytes 14204952
  145.1 3.8 fusion.1
  148.9 24.5 %all-gather.5.cloned.1.call-done = bf16[2176,1536]{1,0:T(8,128)(2,1)} async-done(((bf16[136,1536]{1,0:T(8,128)(2,1)}), bf16[2176,1536]{1,0:T(8,128)(2,1)}) %all-gather.5.cloned.1.call-update) | async-done | bytes 6684688 | tf_op jit(solution)/shard_map/all_gather | solution.py:110
  173.4 9.4 %copy.31 = bf16[2176,1536]{0,1:T(8,128)(2,1)} copy(bf16[2176,1536]{1,0:T(8,128)(2,1)} %all-gather.5.cloned.1.call-done) | data formatting | bytes 13369344 | tf_op jit(solution)/shard_map/all_gather | solution.py:110
  182.7 10.4 %fusion.15 = bf16[136,12,128]{2,0,1:T(8,128)(2,1)S(1)} fusion(bf16[2176,12,128]{0,2,1:T(8,128)(2,1)} %bitcast.79, f32[12,136,2176]{2,1,0:T(8,128)} %copy-done.2, f32[12,136]{1,0:T(8,128)S(1)} %broadcast_maximum_fusion, pred[2176]{0:T(1024)(128)(4,1)S(1)} %broadcast_in_dim.67, f32[136,12]{0,1:T(8,128)S(1)} %bitcast.89), kind=kOutput, calls=%fused_computation.17 | convolution fusion | flops 927289344 | bytes 21322624 | tf_op jit(solution)/shard_map/hqk,khd->hqd/dot_general | solution.py:50
  193.5 8.0 %fusion.19 = f32[3072,1536]{1,0:T(8,128)} fusion(bf16[128,1536]{0,1:T(8,128)(2,1)S(1)} %bitcast.81, bf16[1,128,3072]{2,1,0:T(8,128)(2,1)S(1)} %copy-done.3, f32[3072]{0:T(1024)S(1)} %bitcast.84), kind=kOutput, calls=%fused_computation.19 | convolution fusion | flops 1209139200 | bytes 20066304 | tf_op jit(solution)/shard_map/dot_general | solution.py:133
  202.4 6.2 %fusion.6 = bf16[1,128,1536]{2,1,0:T(8,128)(2,1)} fusion(bf16[3072,1536]{1,0:T(8,128)(2,1)} %param.23, bf16[1,128,3072]{2,1,0:T(8,128)(2,1)} %param.25, f32[3072]{0:T(1024)S(1)} %bitcast.85), kind=kOutput, calls=%fused_computation.9 | convolution fusion | flops 1209335808 | bytes 10629120 | tf_op jit(solution)/shard_map/dot_general | solution.py:129
  208.8 5.4 %fusion.8 = (f32[3072]{0:T(1024)S(1)}, bf16[1,128,3072]{2,1,0:T(8,128)(2,1)}) fusion(bf16[1,128,3072]{2,1,0:T(8,128)(2,1)} %param.25, f32[3072]{0:T(1024)S(1)} %bitcast.86, bf16[128,1536]{0,1:T(8,128)(2,1)} %bitcast.82, bf16[3072,1536]{1,0:T(8,128)(2,1)S(1)} %bitcast.77), kind=kOutput, calls=%fused_computation.13 | convolution fusion | flops 1209922560 | bytes 11427840 | tf_op jit(solution)/shard_map/dot_general | solution.py:121
  214.2 55.7 %all-reduce.2 = f32[3072]{0:T(1024)S(1)} all-reduce(f32[3072]{0:T(1024)S(1)} %get-tuple-element.7), channel_id=5, replica_groups=mesh['dp'=8,'seq'=16] {'seq'}, use_global_device_ids=true, to_apply=%region_9.10.clone | all-reduce | flops 3072 | bytes 24576
  270.5 1.4 fusion.37
  271.9 167.9 %reduce-scatter.5.cloned.1.call-done = f32[24,1536]{1,0:T(8,128)} async-done(((f32[3072,1536]{1,0:T(8,128)}), f32[24,1536]{1,0:T(8,128)}) %reduce-scatter.5.cloned.1.call-update) | async-done | bytes 147472 | tf_op jit(solution)/shard_map/reduce_scatter | solution.py:132
  (53 shorter events, 3.3 us)
Async XLA Ops:
  7.2 3.9 copy-start
  7.2 77.2 %copy-start.9 = (s32[1,128]{1,0:T(1,128)S(1)}, s32[1,128]{1,0:T(1,128)}, u32[]{:S(2)}) copy-start(s32[1,128]{1,0:T(1,128)} %param.17) | copy-start | bytes 1540
  7.2 76.3 %copy-start.7 = (bf16[1,128,1536]{2,1,0:T(8,128)(2,1)S(1)}, bf16[1,128,1536]{2,1,0:T(8,128)(2,1)}, u32[]{:S(2)}) copy-start(bf16[1,128,1536]{2,1,0:T(8,128)(2,1)} %param.22) | copy-start | bytes 1179652
  7.2 77.4 %copy-start.8 = (bf16[1,128,1536]{2,1,0:T(8,128)(2,1)S(1)}, bf16[1,128,1536]{2,1,0:T(8,128)(2,1)}, u32[]{:S(2)}) copy-start(bf16[1,128,1536]{2,1,0:T(8,128)(2,1)} %param.20) | copy-start | bytes 1179652
  7.2 73.2 %reduce-scatter.3.cloned.1.call-start = ((), (), s32[]{:S(2)}) async-start(), calls=%async_computation.2 | async-start | bytes 2506752 | tf_op jit(solution)/shard_map/reduce_scatter | solution.py:89
  13.7 112.2 %all-gather.3.cloned.1.call-start = ((), (), s32[]{:S(2)}) async-start(), calls=%async_computation.3 | async-start | bytes 7102464 | tf_op jit(solution)/shard_map/all_gather | solution.py:109
  83.4 89.9 %all-gather.5.cloned.1.call-start = ((), (), s32[]{:S(2)}) async-start(), calls=%async_computation.4 | async-start | bytes 7102464 | tf_op jit(solution)/shard_map/all_gather | solution.py:110
  84.3 355.4 %reduce-scatter.5.cloned.1.call-start = ((), (), s32[]{:S(2)}) async-start(), calls=%async_computation.5 | async-start | bytes 19021824 | tf_op jit(solution)/shard_map/reduce_scatter | solution.py:132
  140.1 5.1 %copy-start.2 = (f32[12,136,2176]{2,1,0:T(8,128)}, f32[12,136,2176]{2,1,0:T(8,128)S(1)}, u32[]{:S(2)}) copy-start(f32[12,136,2176]{2,1,0:T(8,128)S(1)} %get-tuple-element.14) | copy-start | bytes 42614788
  182.7 10.7 %copy-start.3 = (bf16[1,128,3072]{2,1,0:T(8,128)(2,1)S(1)}, bf16[1,128,3072]{2,1,0:T(8,128)(2,1)}, u32[]{:S(2)}) copy-start(bf16[1,128,3072]{2,1,0:T(8,128)(2,1)} %param.25) | copy-start | bytes 2359300
  182.7 10.7 %copy-start.6 = (f32[1,3072]{1,0:T(1,128)S(1)}, f32[1,3072]{1,0:T(1,128)}, u32[]{:S(2)}) copy-start(f32[1,3072]{1,0:T(1,128)} %param.24) | copy-start | bytes 36868
  193.2 8.3 %copy-start.5 = (bf16[136,12,128]{2,0,1:T(8,128)(2,1)}, bf16[136,12,128]{2,0,1:T(8,128)(2,1)S(1)}, u32[]{:S(2)}) copy-start(bf16[136,12,128]{2,0,1:T(8,128)(2,1)S(1)} %fusion.15) | copy-start | bytes 1253380
  193.5 8.1 %copy-start.4 = (bf16[128,12,128]{0,2,1:T(8,128)(2,1)}, bf16[128,12,128]{0,2,1:T(8,128)(2,1)S(1)}, u32[]{:S(2)}) copy-start(bf16[128,12,128]{0,2,1:T(8,128)(2,1)S(1)} %copy.33) | copy-start | bytes 1179652
  201.5 7.1 %slice-start = ((s8[9437184]{0:T(1024)(128)(4,1)}), s8[1048576]{0:T(1024)(128)(4,1)S(1)}, s32[]{:S(2)}) async-start(s8[9437184]{0:T(1024)(128)(4,1)} %bitcast.76), calls=%async_computation.6 | async-start | bytes 2097152
  202.4 6.2 %slice-start.1 = ((s8[9437184]{0:T(1024)(128)(4,1)}), s8[4194304]{0:T(1024)(128)(4,1)S(1)}, s32[]{:S(2)}) async-start(s8[9437184]{0:T(1024)(128)(4,1)} %bitcast.76), calls=%async_computation.7 | async-start | bytes 8388608
  202.4 6.4 %slice-start.2 = ((s8[9437184]{0:T(1024)(128)(4,1)}), s8[4194304]{0:T(1024)(128)(4,1)S(1)}, s32[]{:S(2)}) async-start(s8[9437184]{0:T(1024)(128)(4,1)} %bitcast.76), calls=%async_computation.8 | async-start | bytes 8388608
  202.4 237.4 %copy-start.1 = (bf16[256,4608]{1,0:T(8,128)(2,1)S(1)}, bf16[256,4608]{1,0:T(8,128)(2,1)}, u32[]{:S(2)}) copy-start(bf16[256,4608]{1,0:T(8,128)(2,1)} %param.15) | copy-start | bytes 7077892
Sparse Core Ops, SparseCore 0:
  13.9 66.5 reduce-scatter.2
  83.6 42.3 all-gather.2
  128.2 45.1 all-gather.4
  201.7 238.0 reduce-scatter.4
where the time goes:
time: 447 us; the launch traced here: 446 us
  waiting for transfers between devices  265 us (59%)
  blocking collectives  87.4 us (20%)
  matrix products  37.4 us (8%)
  local copies, waits for them, and re-layouts  29.2 us (7%)
  between operations  16.2 us (4%)
  other arithmetic  10.6 us (2%)
    reduce_scatter x1, waiting for transfers between devices, on_device(): lax.psum_scatter(lax.dot_general(gated_grad, image_attn, (((0,), (0,)), (...  168 us
    unnamed x2, blocking collectives  87.4 us
    all_gather x1, waiting for transfers between devices, on_device(): lax.all_gather(key_rows, 'seq', axis=0, tiled=True)  40.8 us
    reduce_scatter x1, waiting for transfers between devices, on_device(): lax.psum_scatter(partial_proj, 'seq', scatter_dimension=0, tiled=True)  32.1 us
    all_gather x1, waiting for transfers between devices, on_device(): lax.all_gather(value_rows, 'seq', axis=0, tiled=True)  24.5 us
    dot_general x1, matrix products, attend(): jnp.einsum('hqk,khd->hqd', weights_now.astype(jnp.bfloat16), value_heads,...  10.4 us
    all_gather x1, local copies, waits for them, and re-layouts, on_device(): lax.all_gather(value_rows, 'seq', axis=0, tiled=True)  9.37 us
    all_gather x1, local copies, waits for them, and re-layouts, on_device(): lax.all_gather(key_rows, 'seq', axis=0, tiled=True)  9.33 us
  transfers between devices with their start and end apart: 4, of which 4 were waited for; matrix products, arithmetic and copies ran while one was open for 8% of the time, Pallas kernels for 0%

commit v1 on v0

--- a/solution.py
+++ b/solution.py
@@ -1,3 +1,4 @@
+import functools
 import jax
 import jax.numpy as jnp
 from jax import lax
@@ -6,6 +7,19 @@
 DT5 = 4096
 neg_big = -1e30
 eps_norm = 1e-06
+
+
+def refer_signs(xin, in_dim):
+    trail = []
+    for _ in range(lax.axis_size("seq")):
+        trail.append(xin)
+    piece_now = jnp.stack(trail)
+    clean = lax.all_to_all(piece_now, axis_name="seq", split_axis=0, concat_axis=0)
+    formed = jnp.concatenate(clean, axis=in_dim)
+    return formed
+
+
+launch_node = functools.partial(refer_signs, in_dim=0)
 
 
 def head_norm(values_in, gain_vec):
@@ -106,7 +120,7 @@
     running = attend(
         start_state(query_heads),
         query_heads,
-        lax.all_gather(key_rows, "seq", axis=0, tiled=True),
+        launch_node(key_rows),
         lax.all_gather(value_rows, "seq", axis=0, tiled=True),
         usable_all,
     )

time: 447 us -> 512 us (1.15)
  waiting for transfers between devices: 265 us -> 318 us
  local copies, waits for them, and re-layouts: 29.2 us -> 35.4 us
    all_to_all x0 -> x1, waiting for transfers between devices: none -> 116 us  [refer_signs(): lax.all_to_all(piece_now, axis_name='seq', split_axis=0, concat_axis=0)]
    all_gather x1 -> x0, waiting for transfers between devices: 40.8 us -> none  [on_device(): lax.all_gather(key_rows, 'seq', axis=0, tiled=True)]
    all_gather x1, waiting for transfers between devices: 24.5 us -> 0.02 us  [on_device(): lax.all_gather(value_rows, 'seq', axis=0, tiled=True)]
    another operation x0 -> x2, local copies, waits for them, and re-layouts: none -> 16.2 us  [the longest x1 13 us: attend(): key_heads = key_rows.reshape(count_keys, -1, head_size)]
    all_gather x1 -> x0, local copies, waits for them, and re-layouts: 9.33 us -> none  [on_device(): lax.all_gather(key_rows, 'seq', axis=0, tiled=True)]
  transfers between devices with their start and end apart: 4 -> 4, of which waited for: 4 -> 3; matrix products, arithmetic and copies ran while one was open for 8% -> 9% of each run, Pallas kernels for 0% -> 0%
where the time goes in v1:
time: 512 us; the launch traced here: 511 us
  waiting for transfers between devices  318 us (62%)
  blocking collectives  84.6 us (17%)
  matrix products  41.7 us (8%)
  local copies, waits for them, and re-layouts  35.4 us (7%)
  between operations  16.2 us (3%)
  other arithmetic  9.78 us (2%)
    reduce_scatter x1, waiting for transfers between devices, on_device(): lax.psum_scatter(lax.dot_general(gated_grad, image_attn, (((0,), (0,)), (...  169 us
    all_to_all x1, waiting for transfers between devices, refer_signs(): lax.all_to_all(piece_now, axis_name='seq', split_axis=0, concat_axis=0)  116 us
    unnamed x2, blocking collectives  84.6 us
    reduce_scatter x1, waiting for transfers between devices, on_device(): lax.psum_scatter(partial_proj, 'seq', scatter_dimension=0, tiled=True)  32.8 us
    another operation x1, local copies, waits for them, and re-layouts, attend(): key_heads = key_rows.reshape(count_keys, -1, head_size)  13 us
    dot_general x1, matrix products, attend(): jnp.einsum('hqk,khd->hqd', weights_now.astype(jnp.bfloat16), value_heads,...  10.4 us
  transfers between devices with their start and end apart: 4, of which 3 were waited for; matrix products, arithmetic and copies ran while one was open for 9% of the time, Pallas kernels for 0%

profile of v1, /device:TPU:0, one launch (start us, length us, event | category | flops | bytes accessed | tf_op | source)
XLA Modules:
  0.0 510.6 jit_solution(6823447556282568487)
XLA Ops:
  8.1 0.7 fusion.39
  8.7 0.7 bitcast_compare_fusion
  9.4 1.6 gather_fusion
  11.0 2.6 fusion.29
  13.7 1.2 dynamic-slice
  15.8 31.7 %all-reduce.1 = f32[128]{0:T(128)S(1)} all-reduce(f32[128]{0:T(128)S(1)} %fusion.28), channel_id=3, replica_groups=mesh['dp'=8,'seq'=16] {'seq'}, use_global_device_ids=true, to_apply=%region_2.3.clone | all-reduce | flops 128 | bytes 1024
  47.6 32.8 %reduce-scatter.3.cloned.1.call-done = f32[8,4608]{1,0:T(8,128)} async-done(((f32[128,4608]{1,0:T(8,128)}), f32[8,4608]{1,0:T(8,128)}) %reduce-scatter.3.cloned.1.call-update) | async-done | bytes 147472 | tf_op jit(solution)/shard_map/reduce_scatter | solution.py:103
  80.3 1.0 broadcast_multiply_fusion
  81.3 1.8 pad_maximum_fusion.1
  83.5 3.2 stack.2
  86.7 4.7 all-to-all-start
  92.1 116.4 %all-to-all-done = bf16[16,136,1536]{2,1,0:T(8,128)(2,1)} async-done(((bf16[16,136,1536]{2,1,0:T(8,128)(2,1)}), bf16[16,136,1536]{2,1,0:T(8,128)(2,1)}, u32[]{:S(2)}, u32[]{:S(2)}) %all-to-all-start) | async-done | bytes 6684704 | tf_op jit(solution)/shard_map/all_to_all | solution.py:17
  208.6 13.0 %reshape_reshape.3 = bf16[2176,12,128]{2,1,0:T(8,128)(2,1)} reshape(bf16[16,136,1536]{2,1,0:T(8,128)(2,1)} %all-to-all-done) | data formatting | bytes 13369344 | tf_op jit(solution)/shard_map/reshape;reshape | solution.py:55
  221.6 9.0 %fusion = (f32[12,136]{1,0:T(8,128)S(1)}, f32[12,136,2176]{2,1,0:T(8,128)S(1)}) fusion(pred[2176]{0:T(1024)(128)(4,1)S(1)} %broadcast_in_dim.67, bf16[2176,12,128]{2,1,0:T(8,128)(2,1)} %reshape_reshape.3, bf16[8,12,128]{2,0,1:T(8,128)(2,1)S(1)} %get-tuple-element.9, bf16[128,12,128]{2,0,1:T(8,128)(2,1)S(1)} %copy.26), kind=kOutput, calls=%fused_computation.3 | convolution fusion | flops 920603008 | bytes 21316096 | tf_op jit(solution)/shard_map/qhd,khd->hqk/dot_general | solution.py:57
  230.6 5.0 copy-done.2
  235.6 3.8 fusion.1
  239.4 9.4 %copy.28 = bf16[2176,1536]{0,1:T(8,128)(2,1)} copy(bf16[2176,1536]{1,0:T(8,128)(2,1)} %all-gather.2.cloned.1.call-done) | data formatting | bytes 13369344 | tf_op jit(solution)/shard_map/all_gather | solution.py:124
  248.8 10.4 %fusion.17 = bf16[136,12,128]{2,0,1:T(8,128)(2,1)S(1)} fusion(bf16[2176,12,128]{0,2,1:T(8,128)(2,1)} %bitcast.76, f32[12,136,2176]{2,1,0:T(8,128)} %copy-done.2, f32[12,136]{1,0:T(8,128)S(1)} %broadcast_maximum_fusion, pred[2176]{0:T(1024)(128)(4,1)S(1)} %broadcast_in_dim.67, f32[136,12]{0,1:T(8,128)S(1)} %bitcast.86), kind=kOutput, calls=%fused_computation.19 | convolution fusion | flops 927289344 | bytes 21322624 | tf_op jit(solution)/shard_map/hqk,khd->hqd/dot_general | solution.py:64
  259.6 8.1 %fusion.21 = f32[3072,1536]{1,0:T(8,128)} fusion(bf16[128,1536]{0,1:T(8,128)(2,1)S(1)} %bitcast.78, bf16[1,128,3072]{2,1,0:T(8,128)(2,1)S(1)} %copy-done.3, f32[3072]{0:T(1024)S(1)} %bitcast.81), kind=kOutput, calls=%fused_computation.21 | convolution fusion | flops 1209139200 | bytes 20066304 | tf_op jit(solution)/shard_map/dot_general | solution.py:147
  268.6 6.2 %fusion.8 = bf16[1,128,1536]{2,1,0:T(8,128)(2,1)} fusion(bf16[3072,1536]{1,0:T(8,128)(2,1)} %param.23, bf16[1,128,3072]{2,1,0:T(8,128)(2,1)} %param.25, f32[3072]{0:T(1024)S(1)} %bitcast.82), kind=kOutput, calls=%fused_computation.11 | convolution fusion | flops 1209335808 | bytes 10629120 | tf_op jit(solution)/shard_map/dot_general | solution.py:143
  275.0 5.4 %fusion.10 = (f32[3072]{0:T(1024)S(1)}, bf16[1,128,3072]{2,1,0:T(8,128)(2,1)}) fusion(bf16[1,128,3072]{2,1,0:T(8,128)(2,1)} %param.25, f32[3072]{0:T(1024)S(1)} %bitcast.83, bf16[128,1536]{0,1:T(8,128)(2,1)} %bitcast.79, bf16[3072,1536]{1,0:T(8,128)(2,1)S(1)} %bitcast.75), kind=kOutput, calls=%fused_computation.15 | convolution fusion | flops 1209922560 | bytes 11427840 | tf_op jit(solution)/shard_map/dot_general | solution.py:135
  280.4 52.9 %all-reduce.2 = f32[3072]{0:T(1024)S(1)} all-reduce(f32[3072]{0:T(1024)S(1)} %get-tuple-element.7), channel_id=5, replica_groups=mesh['dp'=8,'seq'=16] {'seq'}, use_global_device_ids=true, to_apply=%region_9.10.clone | all-reduce | flops 3072 | bytes 24576
  333.9 1.4 fusion.38
  335.3 168.8 %reduce-scatter.5.cloned.1.call-done = f32[24,1536]{1,0:T(8,128)} async-done(((f32[3072,1536]{1,0:T(8,128)}), f32[24,1536]{1,0:T(8,128)}) %reduce-scatter.5.cloned.1.call-update) | async-done | bytes 147472 | tf_op jit(solution)/shard_map/reduce_scatter | solution.py:146
  (57 shorter events, 2.6 us)
Async XLA Ops:
  7.2 3.8 copy-start
  7.2 76.0 %copy-start.10 = (f32[128]{0:T(128)S(1)}, f32[128]{0:T(128)}, u32[]{:S(2)}) copy-start(f32[128]{0:T(128)} %param.18) | copy-start | bytes 1540
  7.2 76.0 %copy-start.9 = (f32[128]{0:T(128)S(1)}, f32[128]{0:T(128)}, u32[]{:S(2)}) copy-start(f32[128]{0:T(128)} %param.19) | copy-start | bytes 1540
  7.2 76.2 %copy-start.7 = (bf16[1,128,1536]{2,1,0:T(8,128)(2,1)S(1)}, bf16[1,128,1536]{2,1,0:T(8,128)(2,1)}, u32[]{:S(2)}) copy-start(bf16[1,128,1536]{2,1,0:T(8,128)(2,1)} %param.21) | copy-start | bytes 1179652
  7.2 73.1 %reduce-scatter.3.cloned.1.call-start = ((), (), s32[]{:S(2)}) async-start(), calls=%async_computation.3 | async-start | bytes 2506752 | tf_op jit(solution)/shard_map/reduce_scatter | solution.py:103
  13.6 225.8 %all-gather.2.cloned.1.call-start = ((), (), s32[]{:S(2)}) async-start(), calls=%async_computation.4 | async-start | bytes 7102464 | tf_op jit(solution)/shard_map/all_gather | solution.py:124
  83.4 7.9 %copy-start.11 = (s32[1,128]{1,0:T(1,128)S(1)}, s32[1,128]{1,0:T(1,128)}, u32[]{:S(2)}) copy-start(s32[1,128]{1,0:T(1,128)} %param.17) | copy-start | bytes 1540
  83.4 8.2 %copy-start.8 = (bf16[1,128,1536]{2,1,0:T(8,128)(2,1)S(1)}, bf16[1,128,1536]{2,1,0:T(8,128)(2,1)}, u32[]{:S(2)}) copy-start(bf16[1,128,1536]{2,1,0:T(8,128)(2,1)} %param.20) | copy-start | bytes 1179652
  86.7 121.9 %all-to-all-start = ((bf16[16,136,1536]{2,1,0:T(8,128)(2,1)}), bf16[16,136,1536]{2,1,0:T(8,128)(2,1)}, u32[]{:S(2)}, u32[]{:S(2)}) async-start(bf16[16,136,1536]{2,1,0:T(8,128)(2,1)} %stack.2), calls=%async_computation.1 | async-start | bytes 13369344 | tf_op jit(solution)/shard_map/all_to_all | solution.py:17
  91.3 412.8 %reduce-scatter.5.cloned.1.call-start = ((), (), s32[]{:S(2)}) async-start(), calls=%async_computation.5 | async-start | bytes 19021824 | tf_op jit(solution)/shard_map/reduce_scatter | solution.py:146
  230.6 5.1 copy-start.2
  248.8 10.7 %copy-start.3 = (bf16[1,128,3072]{2,1,0:T(8,128)(2,1)S(1)}, bf16[1,128,3072]{2,1,0:T(8,128)(2,1)}, u32[]{:S(2)}) copy-start(bf16[1,128,3072]{2,1,0:T(8,128)(2,1)} %param.25) | copy-start | bytes 2359300
  248.8 10.7 %copy-start.6 = (f32[1,3072]{1,0:T(1,128)S(1)}, f32[1,3072]{1,0:T(1,128)}, u32[]{:S(2)}) copy-start(f32[1,3072]{1,0:T(1,128)} %param.24) | copy-start | bytes 36868
  259.3 8.4 %copy-start.5 = (bf16[136,12,128]{2,0,1:T(8,128)(2,1)}, bf16[136,12,128]{2,0,1:T(8,128)(2,1)S(1)}, u32[]{:S(2)}) copy-start(bf16[136,12,128]{2,0,1:T(8,128)(2,1)S(1)} %fusion.17) | copy-start | bytes 1253380
  259.6 8.1 %copy-start.4 = (bf16[128,12,128]{0,2,1:T(8,128)(2,1)}, bf16[128,12,128]{0,2,1:T(8,128)(2,1)S(1)}, u32[]{:S(2)}) copy-start(bf16[128,12,128]{0,2,1:T(8,128)(2,1)S(1)} %copy.30) | copy-start | bytes 1179652
  267.7 7.1 %slice-start = ((s8[9437184]{0:T(1024)(128)(4,1)}), s8[1048576]{0:T(1024)(128)(4,1)S(1)}, s32[]{:S(2)}) async-start(s8[9437184]{0:T(1024)(128)(4,1)} %bitcast.74), calls=%async_computation.6 | async-start | bytes 2097152
  268.6 6.2 %slice-start.1 = ((s8[9437184]{0:T(1024)(128)(4,1)}), s8[4194304]{0:T(1024)(128)(4,1)S(1)}, s32[]{:S(2)}) async-start(s8[9437184]{0:T(1024)(128)(4,1)} %bitcast.74), calls=%async_computation.7 | async-start | bytes 8388608
  268.6 6.4 %slice-start.2 = ((s8[9437184]{0:T(1024)(128)(4,1)}), s8[4194304]{0:T(1024)(128)(4,1)S(1)}, s32[]{:S(2)}) async-start(s8[9437184]{0:T(1024)(128)(4,1)} %bitcast.74), calls=%async_computation.8 | async-start | bytes 8388608
  268.6 235.6 %copy-start.1 = (bf16[256,4608]{1,0:T(8,128)(2,1)S(1)}, bf16[256,4608]{1,0:T(8,128)(2,1)}, u32[]{:S(2)}) copy-start(bf16[256,4608]{1,0:T(8,128)(2,1)} %param.15) | copy-start | bytes 7077892
Sparse Core Ops, SparseCore 0:
  13.8 66.5 reduce-scatter.2
  83.3 117.0 all-gather.1
  267.8 236.2 reduce-scatter.4
